TPU v7x, 32 devices: a whole 2x2x4 slice. The times are simulated.
32 devices in a mesh: grp: 2 (over y), tchunk: 2 (over x), ha: 4 (over z), wa: 2 (over core).
Axes of the slice: x: 2, y: 2, z: 4, core: 2. Of those that a mesh axis runs over, the one named last changes fastest.
Arguments:
- features: bfloat16 [32, 32, 16, 192], P(('grp', 'tchunk'), 'ha', 'wa'), parts along dimension 0, may hold values from -6 to 6
- frame_counts: int32 [4], P(('grp', 'tchunk')), parts along dimension 0, may hold values from 0 to 8, as said below
- gain_first: float32 [192], replicated, may hold values from 0.25 to 1.75
- conv_first: bfloat16 [3, 3, 3, 192, 192], replicated, may hold values from -0.078125 to 0.078125
- bias_first: float32 [192], replicated, may hold values from -1.8 to 1.8
- gain_second: float32 [192], replicated, may hold values from 0.25 to 1.75
- conv_second: bfloat16 [3, 3, 3, 192, 192], replicated, may hold values from -0.078125 to 0.078125
- bias_second: float32 [192], replicated, may hold values from -1.8 to 1.8
Outputs:
- decoded: bfloat16 [32, 32, 16, 192], P(('grp', 'tchunk'), 'ha', 'wa'), parts along dimension 0
There are 2 independent parts, one for each index of `grp`. A program takes and returns all parts, laid end to end along the dimension named above; an argument that names none is the same for every part. Nothing has to cross between parts.
Inputs may be any that keep to these rules, and one draw needn't show every extreme that they name: `frame_counts`: in every draw some temporal block has all 8 slots live; any block may have none.
All inputs are finite; a program needn't handle non-finite values.
Results may differ from a plain program's by a relative error of at most 0.0039.
Values may be sent and summed in bfloat16 or wider, within the bound.
A program may use at most 64 MiB of HBM per device.

v0:
```python
import functools

import jax
import jax.numpy as jnp
from jax import lax
from jax.experimental import pallas as pl
from jax.experimental.pallas import tpu as pltpu
from jax.sharding import PartitionSpec as P

epsilon = 1e-06
MESH = pl.DeviceIdType.MESH
DIRS = [(dz, dw) for dz in (-1, 0, 1) for dw in (-1, 0, 1)]
f32, bf16 = jnp.float32, jnp.bfloat16


def silu_norm(values, gain):
    inverse = lax.rsqrt(jnp.mean(values * values, axis=-1, keepdims=True) + epsilon)
    return jax.nn.silu(values * inverse * gain)


def both(*conds):
    out = conds[0]
    for c in conds[1:]:
        out = jnp.logical_and(out, c)
    return out


def kernel(sizes, *refs):
    placed, out, scratch = refs[:8], refs[8], refs[9:]
    n_t, n_z, n_w = sizes
    (cnt_ref, feat, g1, w1, b1, g2, w2, b2) = local = scratch[:8]
    frames, rows, cols, chans = feat.shape
    (lsem, even, odd, acc, cnt_own, cnt_in, carry, carry_col, csend, crecv) = scratch[8:18]
    phases = (scratch[18:30], scratch[30:42])
    me_t, me_z, me_w = lax.axis_index("tchunk"), lax.axis_index("ha"), lax.axis_index("wa")
    loads = [pltpu.make_async_copy(src, dst, lsem.at[i]) for i, (src, dst) in enumerate(zip(placed, local))]
    for i in (1, 2, 4, 5, 7, 3, 6):
        loads[i].start()

    def exists(dz, dw):
        z, w = me_z + dz, me_w + dw
        return both(z >= 0, z < n_z, w >= 0, w < n_w)

    def device(k, dz, dw):
        return {"tchunk": k, "ha": lax.rem(me_z + dz + n_z, n_z), "wa": lax.rem(me_w + dw + n_w, n_w)}

    barrier = pltpu.get_barrier_semaphore()
    expected = jnp.int32(0)
    for k in range(n_t):
        for dz, dw in DIRS:
            there = exists(dz, dw)
            if (dz, dw) == (0, 0):
                there = me_t != k
            expected = expected + there.astype(jnp.int32)

            @pl.when(there)
            def _(k=k, dz=dz, dw=dw):
                pl.semaphore_signal(barrier, inc=1, device_id=device(k, dz, dw), device_id_type=MESH)

    x_of = lax.broadcasted_iota(jnp.int32, (frames, cols, chans), 1)
    t_of = lax.broadcasted_iota(jnp.int32, (frames, cols, chans), 0)
    def near(bufs, dz, dw):
        own, own_col, _, _, row_in, col_in = bufs[:6]
        y, yy = (0, rows + 1) if dz < 0 else (rows - 1, 0)
        s, ss = (0, 1) if dw < 0 else (1, 0)
        if dw == 0:
            return own.at[y, pl.ds(2, frames)], row_in.at[1 if dz < 0 else 0]
        if dz == 0:
            return own_col.at[s], col_in.at[ss, pl.ds(1, rows)]
        return own_col.at[s, y], col_in.at[ss, yy]

    def far(bufs, slot, dz, dw):
        tail, tail_col, tail_in, tailc_in = bufs[2], bufs[3], bufs[6], bufs[7]
        s, ss = (0, 1) if dw < 0 else (1, 0)
        if dw == 0:
            if dz == 0:
                return tail, tail_in.at[slot, pl.ds(1, rows)]
            y, yy = (0, rows + 1) if dz < 0 else (rows - 1, 0)
            return tail.at[y], tail_in.at[slot, yy]
        return tail_col.at[s], tailc_in.at[slot, ss, 1 - dz]

    def near_copy(bufs, dz, dw, way=1):
        src, dst = near(bufs, dz, dw)
        i = DIRS.index((dz, dw))
        return pltpu.make_async_remote_copy(
            src, dst, bufs[8].at[i], bufs[9].at[i], device_id=device(me_t, way * dz, way * dw), device_id_type=MESH
        )

    def far_copy(bufs, k, slot, dz, dw, way=1):
        src, dst = far(bufs, slot, dz, dw)
        i = DIRS.index((dz, dw))
        return pltpu.make_async_remote_copy(
            src, dst, bufs[10].at[k, i], bufs[11].at[slot, i],
            device_id=device(k, way * dz, way * dw), device_id_type=MESH,
        )

    def count_copy(k, slot):
        return pltpu.make_async_remote_copy(
            cnt_own, cnt_in.at[slot], csend.at[k], crecv.at[slot],
            device_id=device(k, 0, 0), device_id_type=MESH,
        )

    def clear(bufs):
        bufs[0][:, :2] = jnp.zeros((rows, 2, cols, chans), bf16)
        for dz, dw in DIRS:
            if (dz, dw) == (0, 0):
                continue

            @pl.when(jnp.logical_not(exists(-dz, -dw)))
            def _(dz=dz, dw=dw):
                dst = near(bufs, dz, dw)[1]
                dst[...] = jnp.zeros(dst.shape, dst.dtype)
                for k in range(n_t):
                    dst = far(bufs, k, dz, dw)[1]
                    dst[...] = jnp.zeros(dst.shape, dst.dtype)

    def keep(bufs, y, value):
        own, own_col = bufs[0], bufs[1]
        value = jnp.where(live, value, 0.0)
        own[y, 2:] = value.astype(bf16)
        own_col[0, y] = value[:, 0, :].astype(bf16)
        own_col[1, y] = value[:, cols - 1, :].astype(bf16)

    def keep_tail(bufs):
        own, _, tail, tail_col = bufs[:4]
        for f in range(2):
            frame = own[:, count + f].astype(f32)
            tail[:, f] = frame.astype(bf16)
            tail_col[0, f] = frame[:, 0, :].astype(bf16)
            tail_col[1, f] = frame[:, cols - 1, :].astype(bf16)

    def send(bufs, first):
        for k in range(1, n_t):
            @pl.when(me_t < k)
            def _(k=k):
                if first:
                    count_copy(k, me_t).start()
                for dz, dw in DIRS:
                    @pl.when(exists(dz, dw))
                    def _(dz=dz, dw=dw):
                        far_copy(bufs, k, me_t, dz, dw).start()
        for dz, dw in DIRS:
            if (dz, dw) != (0, 0):
                @pl.when(exists(dz, dw))
                def _(dz=dz, dw=dw):
                    near_copy(bufs, dz, dw).start()

    def receive_near(bufs):
        for dz, dw in DIRS:
            if (dz, dw) != (0, 0):
                @pl.when(exists(-dz, -dw))
                def _(dz=dz, dw=dw):
                    near_copy(bufs, dz, dw, -1).wait_recv()

    def receive_far(bufs, first):
        tail_in, tailc_in = bufs[6], bufs[7]
        carry[...] = jnp.zeros(carry.shape, f32)
        carry_col[...] = jnp.zeros(carry_col.shape, f32)
        for k in range(n_t - 1):
            @pl.when(me_t > k)
            def _(k=k):
                if first:
                    count_copy(k, k).wait_recv()
                for dz, dw in DIRS:
                    @pl.when(exists(-dz, -dw))
                    def _(dz=dz, dw=dw):
                        far_copy(bufs, k, k, dz, dw, -1).wait_recv()
                total = cnt_in[k]
                two, one = total > 1.5, total > 0.5

                def merge(ref, index, late0, late1):
                    early0, early1 = ref[index + (0,)], ref[index + (1,)]
                    ref[index + (0,)] = jnp.where(two, late0, jnp.where(one, early1, early0))
                    ref[index + (1,)] = jnp.where(one, late1, early1)

                for yy in range(rows + 2):
                    merge(carry, (yy,), tail_in[k, yy, 0].astype(f32), tail_in[k, yy, 1].astype(f32))
                for s in range(2):
                    for d in range(3):
                        merge(carry_col, (s, d), tailc_in[k, s, d, 0].astype(f32), tailc_in[k, s, d, 1].astype(f32))

    def finish_sends(bufs, first):
        for k in range(1, n_t):
            @pl.when(me_t < k)
            def _(k=k):
                if first:
                    count_copy(k, me_t).wait_send()
                for dz, dw in DIRS:
                    @pl.when(exists(dz, dw))
                    def _(dz=dz, dw=dw):
                        far_copy(bufs, k, me_t, dz, dw).wait_send()
        for dz, dw in DIRS:
            if (dz, dw) != (0, 0):
                @pl.when(exists(dz, dw))
                def _(dz=dz, dw=dw):
                    near_copy(bufs, dz, dw).wait_send()

    def spread(block, col_left, col_right):
        count_t = block.shape[0]
        flat = block.reshape(count_t * cols, chans)
        xi = lax.broadcasted_iota(jnp.int32, block.shape, 1)
        left = pltpu.roll(flat, 1, 0).reshape(block.shape)
        left = jnp.where(xi == 0, jnp.broadcast_to(col_left[:, None, :], block.shape), left)
        right = pltpu.roll(flat, count_t * cols - 1, 0).reshape(block.shape)
        right = jnp.where(xi == cols - 1, jnp.broadcast_to(col_right[:, None, :], block.shape), right)
        return jnp.concatenate(
            [left.reshape(flat.shape), flat, right.reshape(flat.shape)], axis=1
        )

    def place(bufs, yy, block):
        col_in = bufs[5]
        got = spread(block, col_in[0, yy].astype(f32), col_in[1, yy].astype(f32))
        even[yy, 2 * cols :] = got.astype(bf16)
        odd[yy, cols : 2 * cols] = got[:cols].astype(bf16)
        odd[yy, 2 * cols :] = got[cols : (frames - 1) * cols].astype(bf16)

    def place_carry(yy):
        d, at = (0, rows - 1) if yy == 0 else (2, 0) if yy == rows + 1 else (1, yy - 1)
        left = carry_col[0, d, :, pl.ds(at, 1), :].reshape(2, chans)
        right = carry_col[1, d, :, pl.ds(at, 1), :].reshape(2, chans)
        got = spread(carry[yy], left, right)
        even[yy, : 2 * cols] = got.astype(bf16)
        odd[yy, :cols] = got[cols:].astype(bf16)

    def gather(bufs, first):
        own, row_in = bufs[0], bufs[4]
        receive_near(bufs)

        for y in range(rows):
            place(bufs, y + 1, own[y, 2:].astype(f32))

        place(bufs, 0, row_in[0].astype(f32))
        place(bufs, rows + 1, row_in[1].astype(f32))
        receive_far(bufs, first)
        for yy in range(rows + 2):
            place_carry(yy)

    def conv(weights):
        size = frames * cols
        for a in range(3):
            for i in range(3):
                if a == 1:
                    lhs = odd[pl.ds(i, rows)]
                else:
                    lhs = even[pl.ds(i, rows), pl.ds(a * cols, size)]
                part = jnp.dot(
                    lhs.reshape(rows * size, 3 * chans), weights[a * 3 + i], preferred_element_type=f32
                )
                if a + i == 0:
                    acc[...] = part
                else:
                    acc[...] += part

    one, two = phases
    clear(one)
    clear(two)
    for i in (1, 2):
        loads[i].wait()
    count = placed[0][0]
    live = t_of < count
    cnt_own[...] = jnp.full(cnt_own.shape, count.astype(f32), f32)

    for y in range(rows):
        keep(one, y, silu_norm(feat[:, y].astype(f32), g1[...].reshape(1, 1, chans)))

    keep_tail(one)
    pl.semaphore_wait(barrier, expected)
    send(one, True)
    gather(one, True)
    loads[3].wait()
    conv(w1)
    for i in (4, 5, 7):
        loads[i].wait()

    for y in range(rows):
        at = y * frames * cols
        hidden = acc[pl.ds(at, frames * cols)] + b1[...]
        keep(two, y, silu_norm(hidden.reshape(frames, cols, chans), g2[...].reshape(1, 1, chans)))

    keep_tail(two)
    send(two, False)
    gather(two, False)
    loads[6].wait()
    conv(w2)

    for y in range(rows):
        at = y * frames * cols
        result = (acc[pl.ds(at, frames * cols)] + b2[...]).reshape(frames, cols, chans)
        result = feat[:, y].astype(f32) + result
        out[:, y] = jnp.where(live, result, 0.0).astype(bf16)

    finish_sends(one, True)
    finish_sends(two, False)


def shards(sizes, features, frame_counts, gain_first, conv_first, bias_first, gain_second, conv_second, bias_second):
    frames, rows, cols, chans = features.shape
    n_t = sizes[0]
    dma = pltpu.SemaphoreType.DMA
    phase = [
        pltpu.VMEM((rows, frames + 2, cols, chans), bf16),
        pltpu.VMEM((2, rows, frames, chans), bf16),
        pltpu.VMEM((rows, 2, cols, chans), bf16),
        pltpu.VMEM((2, 2, rows, chans), bf16),
        pltpu.VMEM((2, frames, cols, chans), bf16),
        pltpu.VMEM((2, rows + 2, frames, chans), bf16),
        pltpu.VMEM((n_t, rows + 2, 2, cols, chans), bf16),
        pltpu.VMEM((n_t, 2, 3, 2, rows, chans), bf16),
        dma((len(DIRS),)),
        dma((len(DIRS),)),
        dma((n_t, len(DIRS))),
        dma((n_t, len(DIRS))),
    ]
    scratch = [
        pltpu.SMEM((1,), jnp.int32),
        pltpu.VMEM(features.shape, bf16),
        pltpu.VMEM((1, chans), f32),
        pltpu.VMEM((9, 3 * chans, chans), bf16),
        pltpu.VMEM((1, chans), f32),
        pltpu.VMEM((1, chans), f32),
        pltpu.VMEM((9, 3 * chans, chans), bf16),
        pltpu.VMEM((1, chans), f32),
        dma((8,)),
        pltpu.VMEM((rows + 2, (frames + 2) * cols, 3 * chans), bf16),
        pltpu.VMEM((rows + 2, frames * cols, 3 * chans), bf16),
        pltpu.VMEM((rows * frames * cols, chans), f32),
        pltpu.VMEM((cols, chans), f32),
        pltpu.VMEM((n_t, cols, chans), f32),
        pltpu.VMEM((rows + 2, 2, cols, chans), f32),
        pltpu.VMEM((2, 3, 2, rows, chans), f32),
        dma((n_t,)),
        dma((n_t,)),
    ]
    vmem = pl.BlockSpec(memory_space=pltpu.VMEM)
    return pl.pallas_call(
        functools.partial(kernel, sizes),
        out_shape=jax.ShapeDtypeStruct(features.shape, features.dtype),
        in_specs=[pl.BlockSpec(memory_space=pltpu.SMEM)] + [pl.BlockSpec(memory_space=pltpu.HBM)] * 7,
        out_specs=vmem,
        scratch_shapes=scratch + phase + phase,
        compiler_params=pltpu.CompilerParams(
            collective_id=0, has_side_effects=True, vmem_limit_bytes=60 << 20
        ),
    )(
        frame_counts,
        features,
        gain_first.reshape(1, chans),
        conv_first.reshape(9, 3 * chans, chans),
        bias_first.reshape(1, chans),
        gain_second.reshape(1, chans),
        conv_second.reshape(9, 3 * chans, chans),
        bias_second.reshape(1, chans),
    )


def solution(mesh):
    sizes = (mesh.shape["tchunk"], mesh.shape["ha"], mesh.shape["wa"])
    spec = P(("grp", "tchunk"), "ha", "wa", None)
    return jax.shard_map(
        functools.partial(shards, sizes),
        mesh=mesh,
        in_specs=(spec, P(("grp", "tchunk")), P(), P(), P(), P(), P(), P()),
        out_specs=spec,
        check_vma=False,
    )
```

profile of v0, /device:TPU:0, one launch (start us, length us, event | category | flops | bytes accessed | tf_op | source)
XLA Modules:
  0.0 21.7 jit_solution(9458873011356832461)
XLA Ops:
  0.7 19.4 %shard_map.82 = bf16[8,8,8,192]{3,2,1,0:T(8,128)(2,1)} custom-call(s32[1]{0:T(128)S(6)} %copy.10.refs_0_, bf16[8,8,8,192]{3,2,1,0:T(8,128)(2,1)} %refs_1_.1, f32[1,192]{1,0:T(1,128)} %bitcast.8, bf16[9,576,192]{2,1,0:T(8,128)(2,1)} %bitcast.6, f32[1,192]{1,0:T(1,128)} %bitcast.9, f32[1,192]{1,0:T(1,128)} %bitcast.10, bf16[9,576,192]{2,1,0:T(8,128)(2,1)} %bitcast.7, ...), custom_call_target="tpu_custom_call" | custom-call | tf_op jit(solution)/shard_map/pallas_call | solution.py:335
  20.0 1.7 %copy.11 = bf16[8,8,8,192]{3,2,1,0:T(8,128)(2,1)} copy(bf16[8,8,8,192]{3,2,1,0:T(8,128)(2,1)} %shard_map.82) | data formatting | bytes 393216
where the time goes:
time: 21.8 us; the launch traced here: 21.7 us
  Pallas kernels  19.4 us (89%)
  local copies, waits for them, and re-layouts  1.67 us (8%)
  between operations  0.66 us (3%)
    pallas_call x1, Pallas kernels, shards(): pl.pallas_call(functools.partial(kernel, sizes), out_shape=jax.ShapeDtype...  19.4 us
    unnamed x1, local copies, waits for them, and re-layouts  1.67 us

commit v1 on v0

v1 whole, which is shorter than its diff:
```python
import functools

import jax
import jax.numpy as jnp
from jax import lax
from jax.experimental import pallas as pl
from jax.experimental.pallas import tpu as pltpu
from jax.sharding import PartitionSpec as P

epsilon = 1e-06
MESH = pl.DeviceIdType.MESH
LANES = 128
f32, bf16 = jnp.float32, jnp.bfloat16


def silu_norm(values, gain):
    inverse = lax.rsqrt(jnp.mean(values * values, axis=-1, keepdims=True) + epsilon)
    return jax.nn.silu(values * inverse * gain)


def kernel(sizes, *refs):
    placed, out, scratch = refs[:8], refs[8], refs[9:]
    n_t, n_z, n_w = sizes
    cnt_ref, feat_hbm, g1_hbm, w1_hbm, b1_hbm, g2_hbm, w2_hbm, b2_hbm = placed
    (feat, g1, b1, g2, b2, wl1, wc1, ws1, wl2, wc2, ws2, lsem, lo, hc, hs, acc,
     clo, chc, chs, cnt_own, cnt_in, carry, carry_col, csend, crecv) = scratch[:25]
    one, two = scratch[25:37], scratch[37:49]
    F, R, X, C = feat.shape
    H = F // 2
    S = F * X
    T = 2 * X
    me_t, me_z, me_w = lax.axis_index("tchunk"), lax.axis_index("ha"), lax.axis_index("wa")
    left_core = me_w == 0
    has = (me_z > 0, me_z < n_z - 1)
    frame_of = [(g % 2) * H + g // 2 for g in range(F)]

    def load(i, src, dst):
        return pltpu.make_async_copy(src, dst, lsem.at[i])

    def weight_loads(i, w, wl, wc, ws):
        low, high = pl.ds(0, LANES), pl.ds(LANES, C - LANES)
        top, bottom = pl.ds(0, C - LANES), pl.ds(C - LANES, C - LANES)
        return [
            load(i, w.at[:, :, :, low], wl),
            load(i + 1, w.at[0, :, 1, high], wc.at[0, :, top]),
            load(i + 2, w.at[1, :, 1, high], wc.at[0, :, bottom]),
            load(i + 3, w.at[2, :, 1, high], wc.at[1, :, top]),
            load(i + 4, w.at[:, :, 0, high], ws.at[:, :, top]),
            load(i + 5, w.at[:, :, 2, high], ws.at[:, :, bottom]),
        ]

    load_feat = load(0, feat_hbm, feat)
    load_g1 = load(1, g1_hbm, g1)
    load_rest = [load(2, b1_hbm, b1), load(3, g2_hbm, g2), load(4, b2_hbm, b2)]
    load_w1 = weight_loads(5, w1_hbm, wl1, wc1, ws1)
    load_w2 = weight_loads(11, w2_hbm, wl2, wc2, ws2)
    load_feat.start()
    load_g1.start()

    def device(k, dz, flip):
        return {
            "tchunk": k,
            "ha": lax.rem(me_z + dz + n_z, n_z),
            "wa": 1 - me_w if flip else me_w,
        }

    barrier = pltpu.get_barrier_semaphore()
    pl.semaphore_signal(barrier, inc=1, device_id=device(me_t, 0, True), device_id_type=MESH)
    for side in range(2):
        @pl.when(has[side])
        def _(side=side):
            for flip in (False, True):
                pl.semaphore_signal(
                    barrier, inc=1, device_id=device(me_t, 2 * side - 1, flip), device_id_type=MESH
                )
    for k in range(n_t):
        @pl.when(me_t != k)
        def _(k=k):
            pl.semaphore_signal(barrier, inc=1, device_id=device(k, 0, False), device_id_type=MESH)
    expected = n_t + 2 * has[0].astype(jnp.int32) + 2 * has[1].astype(jnp.int32)

    for c in load_w1 + load_rest + load_w2:
        c.start()

    def near(bufs, which, way=1):
        rows, col_out, row_in, col_in, _, _, _, _, ssem, rsem = bufs[:10]
        if which == 4:
            src, dst, dz, flip = col_out, col_in.at[pl.ds(1, R)], 0, True
        else:
            side, flip = which % 2, which >= 2
            dz = 2 * side - 1
            y, yy = (0, R + 1) if side == 0 else (R - 1, 0)
            if flip:
                src, dst = col_out.at[y], col_in.at[yy]
            else:
                src, dst = rows.at[y], row_in.at[1 - side]
        return pltpu.make_async_remote_copy(
            src, dst, ssem.at[which], rsem.at[which], device_id=device(me_t, way * dz, flip), device_id_type=MESH
        )

    def far(bufs, k, slot, which):
        _, _, _, _, tail, tailc, tail_in, tailc_in, _, _, ssem, rsem = bufs
        if which == 0:
            src, dst = tail.at[pl.ds(1, R)], tail_in.at[slot, pl.ds(1, R)]
        elif which == 3:
            src, dst = tailc, tailc_in.at[slot]
        else:
            yy = 0 if which == 1 else R + 1
            src, dst = tail.at[yy], tail_in.at[slot, yy]
        return pltpu.make_async_remote_copy(
            src, dst, ssem.at[k, which], rsem.at[slot, which],
            device_id=device(k, 0, False), device_id_type=MESH,
        )

    def count_copy(k, slot):
        return pltpu.make_async_remote_copy(
            cnt_own, cnt_in.at[slot], csend.at[k], crecv.at[slot],
            device_id=device(k, 0, False), device_id_type=MESH,
        )

    def later(act):
        for k in range(1, n_t):
            @pl.when(me_t < k)
            def _(k=k):
                act(k)

    def clear(bufs):
        row_in, col_in = bufs[2], bufs[3]
        for side in range(2):
            @pl.when(jnp.logical_not(has[side]))
            def _(side=side):
                row_in[side] = jnp.zeros((S, C), bf16)
                col_in[side * (R + 1)] = jnp.zeros((F, C), bf16)

    clear(one)
    clear(two)
    for wc in (wc1, wc2):
        wc[1, :, C - LANES :] = jnp.zeros((3, C - LANES, C), bf16)

    count = cnt_ref[0]
    cnt_own[...] = jnp.full(cnt_own.shape, count.astype(f32), f32)
    group = lax.broadcasted_iota(jnp.int32, (F, X, C), 0)
    live = lax.rem(group, 2) * H + group // 2 < count
    xi = lax.broadcasted_iota(jnp.int32, (F, X, C), 1)

    def tail_of(v):
        got = []
        for f in range(2):
            t = jnp.zeros((X, C), f32)
            for g in range(F):
                t = jnp.where(count - 2 + f == frame_of[g], v[g], t)
            got.append(t)
        return jnp.concatenate(got, axis=0).astype(bf16)

    def keep(bufs, y, v):
        rows, col_out, tail = bufs[0], bufs[1], bufs[4]
        v = jnp.where(live, v.reshape(F, X, C), 0.0)
        rows[y] = v.reshape(S, C).astype(bf16)
        col_out[y] = jnp.where(left_core, v[:, X - 1, :], v[:, 0, :]).astype(bf16)
        if n_t > 1:
            tail[y + 1] = tail_of(v)

    def shifted(v, col):
        index = lax.broadcasted_iota(jnp.int32, v.shape, 1)
        none = jnp.zeros(col.shape, f32)
        lcol = jnp.where(left_core, none, col)
        rcol = jnp.where(left_core, col, none)
        left = jnp.where(index == 0, jnp.broadcast_to(lcol[:, None, :], v.shape), pltpu.roll(v, 1, 1))
        right = jnp.where(index == X - 1, jnp.broadcast_to(rcol[:, None, :], v.shape), pltpu.roll(v, X - 1, 1))
        return left, v, right

    def assemble(yy, v, col):
        zero = jnp.zeros((X, C), f32)
        made = []
        for j, b in enumerate(shifted(v.reshape(F, X, C), col)):
            front = jnp.concatenate([zero, b[2 * (H - 2)], zero, b[2 * (H - 1)]], axis=0)
            t = jnp.concatenate([front, b.reshape(S, C)], axis=0).astype(bf16)
            lo[j, yy] = t[:, :LANES]
            made.append(t[:, LANES:])
        hs[yy] = jnp.concatenate([made[0], made[2]], axis=1)
        after = jnp.concatenate([made[1][T:], jnp.zeros((T, C - LANES), bf16)], axis=0)
        hc[yy] = jnp.concatenate([made[1], after], axis=1)

    def conv(i, y0, y1, wl, wc, ws, first=False):
        n = y1 - y0

        def take(ref, a):
            return ref[pl.ds(y0 + i, n), pl.ds(a * T, S)].reshape(n * S, LANES)

        lhs = [take(lo.at[j], a) for a in range(3) for j in range(3)]
        lhs += [take(hc, 0), take(hc, 2)] + [take(hs, a) for a in range(3)]
        rhs = [wl[a, i].reshape(3 * LANES, C) for a in range(3)]
        rhs += [wc[0, i], wc[1, i]] + [ws[a, i] for a in range(3)]
        part = jnp.dot(jnp.concatenate(lhs, axis=1), jnp.concatenate(rhs, axis=0), preferred_element_type=f32)
        at = pl.ds(y0 * S, n * S)
        if first:
            acc[at] = part
        else:
            acc[at] += part

    def early(bufs, first):
        rows, col_in = bufs[0], bufs[3]
        near(bufs, 4).wait_recv()
        for y in range(R):
            assemble(y + 1, rows[y].astype(f32), col_in[y + 1].astype(f32))

    def main(wl, wc, ws):
        conv(1, 0, R, wl, wc, ws, True)
        conv(0, 1, R, wl, wc, ws)
        conv(2, 0, R - 1, wl, wc, ws)

    def edges(bufs, wl, wc, ws):
        row_in, col_in, tail, tailc = bufs[2], bufs[3], bufs[4], bufs[5]
        for side in range(2):
            @pl.when(has[side])
            def _(side=side):
                near(bufs, 1 - side, -1).wait_recv()
                near(bufs, 3 - side, -1).wait_recv()
        if n_t > 1:
            tail[0] = tail_of(row_in[0].astype(f32).reshape(F, X, C))
            tail[R + 1] = tail_of(row_in[1].astype(f32).reshape(F, X, C))
            at = lax.broadcasted_iota(jnp.int32, (F, C), 0)
            of_row = lax.rem(at, 2) * H + at // 2
            index = lax.broadcasted_iota(jnp.int32, (tailc.shape[1], C), 0)
            for f in range(2):
                t = jnp.zeros(index.shape, f32)
                for yy in range(R + 2):
                    only = jnp.where(of_row == count - 2 + f, col_in[yy].astype(f32), 0.0)
                    t = jnp.where(index == yy, jnp.sum(only, axis=0, keepdims=True), t)
                tailc[f] = t.astype(bf16)

            def go(k):
                for which in (1, 2, 3):
                    far(bufs, k, me_t, which).start()

            later(go)
        for yy in (0, R + 1):
            assemble(yy, row_in[min(yy, 1)].astype(f32), col_in[yy].astype(f32))
        conv(0, 0, 1, wl, wc, ws)
        conv(2, R - 1, R, wl, wc, ws)

    def before(bufs, first, wl, wc, ws):
        tail_in, tailc_in = bufs[6], bufs[7]
        carry[...] = jnp.zeros(carry.shape, f32)
        carry_col[...] = jnp.zeros(carry_col.shape, f32)
        for k in range(n_t - 1):
            @pl.when(me_t > k)
            def _(k=k):
                if first:
                    count_copy(k, k).wait_recv()
                for which in range(4):
                    far(bufs, k, k, which).wait_recv()
                total = cnt_in[k]
                wide = jnp.concatenate([total] * (carry_col.shape[1] // X), axis=0)

                def merge(total, early0, early1, late0, late1):
                    both, some = total > 1.5, total > 0.5
                    return (
                        jnp.where(both, late0, jnp.where(some, early1, early0)),
                        jnp.where(some, late1, early1),
                    )

                for yy in range(R + 2):
                    late = tail_in[k, yy].astype(f32)
                    got = merge(total, carry[yy, :X], carry[yy, X:], late[:X], late[X:])
                    carry[yy] = jnp.concatenate(got, axis=0)
                got = merge(
                    wide, carry_col[0], carry_col[1], tailc_in[k, 0].astype(f32), tailc_in[k, 1].astype(f32)
                )
                carry_col[0] = got[0]
                carry_col[1] = got[1]

        cols = (carry_col[0], carry_col[1])
        zero = jnp.zeros((X, C), f32)
        for yy in range(R + 2):
            col = jnp.concatenate([c[yy : yy + 1] for c in cols], axis=0)
            made, mid = [], None
            for j, b in enumerate(shifted(carry[yy].reshape(2, X, C), col)):
                t = jnp.concatenate([b[0], b[1], b[1], zero], axis=0).astype(bf16)
                clo[j, yy] = t[:, :LANES]
                made.append(t[:, LANES:])
            chs[yy] = jnp.concatenate([made[0], made[2]], axis=1)
            chc[yy] = jnp.concatenate([made[1][:T], made[1][T:]], axis=1)
        lhs, rhs = [], []
        for i in range(3):
            for a in range(2):
                for j in range(3):
                    lhs.append(clo[j, pl.ds(i, R), pl.ds(a * T, T)].reshape(R * T, LANES))
                lhs.append(chs[pl.ds(i, R), pl.ds(a * T, T)].reshape(R * T, LANES))
                rhs += [wl[a, i].reshape(3 * LANES, C), ws[a, i]]
            lhs.append(chc[pl.ds(i, R)].reshape(R * T, LANES))
            rhs.append(wc[0, i])
        part = jnp.dot(jnp.concatenate(lhs, axis=1), jnp.concatenate(rhs, axis=0), preferred_element_type=f32)
        for y in range(R):
            for f in range(2):
                acc[pl.ds(y * S + f * T, X)] += part[y * T + f * X : y * T + (f + 1) * X]

    def phase(bufs, first, values, wl, wc, ws, loads):
        for y in (0, R - 1):
            keep(bufs, y, values(y))
        if first:
            pl.semaphore_wait(barrier, expected)
        for side in range(2):
            @pl.when(has[side])
            def _(side=side):
                near(bufs, side).start()
                near(bufs, 2 + side).start()
        for y in range(1, R - 1):
            keep(bufs, y, values(y))
        near(bufs, 4).start()

        def go(k):
            if first:
                count_copy(k, me_t).start()
            far(bufs, k, me_t, 0).start()

        later(go)
        early(bufs, first)
        for c in loads:
            c.wait()
        main(wl, wc, ws)
        edges(bufs, wl, wc, ws)
        if n_t > 1:
            @pl.when(me_t > 0)
            def _():
                before(bufs, first, wl, wc, ws)

    def finish(bufs, first):
        near(bufs, 4).wait_send()
        for side in range(2):
            @pl.when(has[side])
            def _(side=side):
                near(bufs, side).wait_send()
                near(bufs, 2 + side).wait_send()

        def done(k):
            if first:
                count_copy(k, me_t).wait_send()
            for which in range(4):
                far(bufs, k, me_t, which).wait_send()

        later(done)

    load_feat.wait()
    load_g1.wait()

    def in_groups(y):
        return jnp.concatenate([feat[t, y].astype(f32) for t in frame_of], axis=0)

    phase(one, True, lambda y: silu_norm(in_groups(y), g1[...]), wl1, wc1, ws1, load_w1)
    for c in load_rest:
        c.wait()

    def hidden(y):
        return silu_norm(acc[pl.ds(y * S, S)] + b1[...], g2[...])

    phase(two, False, hidden, wl2, wc2, ws2, load_w2)
    for y in range(R):
        result = acc[pl.ds(y * S, S)] + b2[...]
        for g in range(F):
            t = frame_of[g]
            value = feat[t, y].astype(f32) + result[g * X : (g + 1) * X]
            out[t, y] = jnp.where(live[g], value, 0.0).astype(bf16)
    finish(one, True)
    finish(two, False)


def shards(sizes, features, frame_counts, gain_first, conv_first, bias_first, gain_second, conv_second, bias_second):
    F, R, X, C = features.shape
    n_t, n_z, n_w = sizes
    assert n_w == 2 and F % 2 == 0 and F >= 4 and X == 8 and 2 * (C - LANES) == LANES and R >= 2
    H = F // 2
    S, T = F * X, 2 * X
    wide = -(-(R + 2) // 16) * 16
    dma = pltpu.SemaphoreType.DMA
    V = pltpu.VMEM
    phase = [
        V((R, S, C), bf16),
        V((R, F, C), bf16),
        V((2, S, C), bf16),
        V((R + 2, F, C), bf16),
        V((R + 2, T, C), bf16),
        V((2, wide, C), bf16),
        V((n_t, R + 2, T, C), bf16),
        V((n_t, 2, wide, C), bf16),
        dma((5,)),
        dma((5,)),
        dma((n_t, 4)),
        dma((n_t, 4)),
    ]
    weights = [V((3, 3, 3, LANES, C), bf16), V((2, 3, LANES, C), bf16), V((3, 3, LANES, C), bf16)]
    scratch = [
        V(features.shape, bf16),
        V((1, C), f32),
        V((1, C), f32),
        V((1, C), f32),
        V((1, C), f32),
        *weights,
        *weights,
        dma((17,)),
        V((3, R + 2, (H + 2) * T, LANES), bf16),
        V((R + 2, (H + 2) * T, LANES), bf16),
        V((R + 2, (H + 2) * T, LANES), bf16),
        V((R * S, C), f32),
        V((3, R + 2, 2 * T, LANES), bf16),
        V((R + 2, T, LANES), bf16),
        V((R + 2, 2 * T, LANES), bf16),
        V((X, C), f32),
        V((n_t, X, C), f32),
        V((R + 2, T, C), f32),
        V((2, wide, C), f32),
        dma((n_t,)),
        dma((n_t,)),
    ]
    return pl.pallas_call(
        functools.partial(kernel, sizes),
        out_shape=pltpu.VMEM(features.shape, features.dtype),
        in_specs=[pl.BlockSpec(memory_space=pltpu.SMEM)] + [pl.BlockSpec(memory_space=pltpu.HBM)] * 7,
        out_specs=pl.BlockSpec(memory_space=pltpu.VMEM),
        scratch_shapes=scratch + phase + phase,
        compiler_params=pltpu.CompilerParams(
            collective_id=0, has_side_effects=True, vmem_limit_bytes=58 << 20
        ),
    )(
        frame_counts,
        features,
        gain_first.reshape(1, C),
        conv_first,
        bias_first.reshape(1, C),
        gain_second.reshape(1, C),
        conv_second,
        bias_second.reshape(1, C),
    )


def solution(mesh):
    sizes = (mesh.shape["tchunk"], mesh.shape["ha"], mesh.shape["wa"])
    spec = P(("grp", "tchunk"), "ha", "wa", None)
    return jax.shard_map(
        functools.partial(shards, sizes),
        mesh=mesh,
        in_specs=(spec, P(("grp", "tchunk")), P(), P(), P(), P(), P(), P()),
        out_specs=spec,
        check_vma=False,
    )
```

time: 21.8 us -> 15.5 us (0.71)
  the two profiles are of different devices: /device:TPU:0 before, /device:TPU:15 now
where the time goes in v1:
time: 15.5 us; the launch traced here: 15.3 us
  Pallas kernels  13.9 us (90%)
  local copies, waits for them, and re-layouts  0.71 us (5%)
  between operations  0.66 us (4%)
    pallas_call x1, Pallas kernels, shards(): pl.pallas_call(functools.partial(kernel, sizes), out_shape=pltpu.VMEM(fea...  13.9 us
    unnamed x1, local copies, waits for them, and re-layouts  0.71 us

profile of v1, /device:TPU:15, one launch (start us, length us, event | category | flops | bytes accessed | tf_op | source)
XLA Modules:
  0.0 15.3 jit_solution(3694241213252796539)
XLA Ops:
  0.7 13.9 %shard_map.82 = bf16[8,8,8,192]{3,2,1,0:T(8,128)(2,1)S(1)} custom-call(s32[1]{0:T(128)S(6)} %copy.11.refs_0_, bf16[8,8,8,192]{3,2,1,0:T(8,128)(2,1)} %refs_1_.1, f32[1,192]{1,0:T(1,128)} %bitcast.4, bf16[3,3,3,192,192]{4,3,2,1,0:T(8,128)(2,1)} %refs_3_.1, f32[1,192]{1,0:T(1,128)} %bitcast.5, f32[1,192]{1,0:T(1,128)} %bitcast.6, ...), custom_call_target="tpu_custom_call" | custom-call | tf_op jit(solution)/shard_map/pallas_call | solution.py:415
  14.6 0.7 %copy.10 = bf16[8,8,8,192]{3,2,1,0:T(8,128)(2,1)} copy(bf16[8,8,8,192]{3,2,1,0:T(8,128)(2,1)S(1)} %shard_map.82) | data formatting | bytes 393216

commit v2 on v1

v2 whole, which is shorter than its diff:
```python
import functools

import jax
import jax.numpy as jnp
from jax import lax
from jax.experimental import pallas as pl
from jax.experimental.pallas import tpu as pltpu
from jax.sharding import PartitionSpec as P

epsilon = 1e-06
MESH = pl.DeviceIdType.MESH
LANES = 128
f32, bf16 = jnp.float32, jnp.bfloat16


def silu_norm(values, gain):
    inverse = lax.rsqrt(jnp.mean(values * values, axis=-1, keepdims=True) + epsilon)
    return jax.nn.silu(values * inverse * gain)


def kernel(sizes, *refs):
    placed, out, scratch = refs[:8], refs[8], refs[9:]
    n_t, n_z, n_w = sizes
    cnt_ref, feat_hbm, g1_hbm, w1_hbm, b1_hbm, g2_hbm, w2_hbm, b2_hbm = placed
    (feat, g1, b1, g2, b2, wl1, wc1, ws1, wl2, wc2, ws2, lsem, lo, hc, hs, acc,
     clo, chc, chs, cnt_own, cnt_in, carry, carry_col,
     raw_in, rows1, col_out1, col_in1, tail1, tailc1, tail_in1, tailc_in1, tailhc_in,
     rows2, col_out2, col_in2, tail2, tailc2, tail_in2, tailc_in2,
     nsend, nrecv, fsend, frecv, up, over, over_up) = scratch
    F, R, X, C = feat.shape
    H = F // 2
    S = F * X
    T = 2 * X
    me_t, me_z, me_w = lax.axis_index("tchunk"), lax.axis_index("ha"), lax.axis_index("wa")
    left_core = me_w == 0
    has = (me_z > 0, me_z < n_z - 1)
    frame_of = [(g % 2) * H + g // 2 for g in range(F)]

    def load(i, src, dst):
        return pltpu.make_async_copy(src, dst, lsem.at[i])

    def weight_loads(i, w, wl, wc, ws):
        low, high = pl.ds(0, LANES), pl.ds(LANES, C - LANES)
        top, bottom = pl.ds(0, C - LANES), pl.ds(C - LANES, C - LANES)
        return [
            load(i, w.at[:, :, :, low], wl),
            load(i + 1, w.at[0, :, 1, high], wc.at[0, :, top]),
            load(i + 2, w.at[1, :, 1, high], wc.at[0, :, bottom]),
            load(i + 3, w.at[2, :, 1, high], wc.at[1, :, top]),
            load(i + 4, w.at[:, :, 0, high], ws.at[:, :, top]),
            load(i + 5, w.at[:, :, 2, high], ws.at[:, :, bottom]),
        ]

    load_feat = load(0, feat_hbm, feat)
    load_g1 = load(1, g1_hbm, g1)
    load_rest = [load(2, b1_hbm, b1), load(3, g2_hbm, g2), load(4, b2_hbm, b2)]
    load_w1 = weight_loads(5, w1_hbm, wl1, wc1, ws1)
    load_w2 = weight_loads(11, w2_hbm, wl2, wc2, ws2)
    load_feat.start()
    load_g1.start()

    def device(k, dz, flip):
        return {
            "tchunk": k,
            "ha": lax.rem(me_z + dz + n_z, n_z),
            "wa": 1 - me_w if flip else me_w,
        }

    barrier = pltpu.get_barrier_semaphore()

    def greet(k, dz, flip):
        pl.semaphore_signal(barrier, inc=1, device_id=device(k, dz, flip), device_id_type=MESH)

    greet(me_t, 0, True)

    @pl.when(has[1])
    def _():
        greet(me_t, 1, False)
        greet(me_t, 1, True)

    for k in range(1, n_t):
        @pl.when(me_t < k)
        def _(k=k):
            greet(k, 0, False)

    expected = 1 + 2 * has[0].astype(jnp.int32) + me_t

    def tell(sem, k, dz, flip):
        pl.semaphore_signal(sem, inc=1, device_id=device(k, dz, flip), device_id_type=MESH)

    def tell_lower(sems):
        for k in range(1, n_t):
            @pl.when(me_t == k)
            def _(k=k):
                for lower in range(k):
                    tell(sems.at[k], lower, 0, False)

    for c in load_w1 + load_rest + load_w2:
        c.start()

    def remote(src, dst, ssem, rsem, to):
        return pltpu.make_async_remote_copy(src, dst, ssem, rsem, device_id=to, device_id_type=MESH)

    def row_copy(side, way=1):
        src = feat_hbm.at[:, pl.ds((R - 2) * side, 2)]
        return remote(src, raw_in.at[1 - side], nsend.at[side], nrecv.at[side], device(me_t, way * (2 * side - 1), False))

    def corner_copy(side, way=1):
        src = col_out1.at[pl.ds((R - 2) * side, 2)]
        dst = col_in1.at[pl.ds(0 if side else R + 2, 2)]
        i = 2 + side
        return remote(src, dst, nsend.at[i], nrecv.at[i], device(me_t, way * (2 * side - 1), True))

    def col_copy(first):
        src, dst, i = (col_out1, col_in1.at[pl.ds(2, R)], 4) if first else (col_out2, col_in2, 5)
        return remote(src, dst, nsend.at[i], nrecv.at[i], device(me_t, 0, True))

    def far(k, slot, i, way=1):
        src, dst, dz, flip = (
            (tail1, tail_in1.at[slot, pl.ds(0, R)], 0, False),
            (tailc1, tailc_in1.at[slot], 0, True),
            (tail1.at[pl.ds(0, 2)], tail_in1.at[slot, pl.ds(R + 2, 2)], -1, False),
            (tailc1, tailhc_in.at[slot, 1], -1, True),
            (tail1.at[pl.ds(R - 2, 2)], tail_in1.at[slot, pl.ds(R, 2)], 1, False),
            (tailc1, tailhc_in.at[slot, 0], 1, True),
            (tail2, tail_in2.at[slot], 0, False),
            (tailc2, tailc_in2.at[slot], 0, True),
            (cnt_own, cnt_in.at[slot], 0, False),
        )[i]
        return remote(src, dst, fsend.at[k, i], frecv.at[slot, i], device(k, way * dz, flip))

    def later(act):
        for k in range(1, n_t):
            @pl.when(me_t < k)
            def _(k=k):
                act(k)

    def aside(act, side):
        @pl.when(has[side])
        def _():
            for i in (2, 3) if side == 0 else (4, 5):
                act(i)

    for side in range(2):
        @pl.when(jnp.logical_not(has[side]))
        def _(side=side):
            raw_in[side] = jnp.zeros((F, 2, X, C), bf16)
            col_in1[pl.ds(side * (R + 2), 2)] = jnp.zeros((2, F, C), bf16)
            for k in range(n_t - 1):
                tail_in1[k, pl.ds(R + 2 * side, 2)] = jnp.zeros((2, T, C), bf16)
                tailhc_in[k, side] = jnp.zeros((2, R, C), bf16)
    for wc in (wc1, wc2):
        wc[1, :, C - LANES :] = jnp.zeros((3, C - LANES, C), bf16)

    count = cnt_ref[0]
    cnt_own[...] = jnp.full(cnt_own.shape, count.astype(f32), f32)
    group = lax.broadcasted_iota(jnp.int32, (F, X, C), 0)
    live = lax.rem(group, 2) * H + group // 2 < count

    def edge(v, at=0):
        return jnp.where(left_core, v[:, at + X - 1, :], v[:, at, :])

    def tail_of(v):
        got = []
        for f in range(2):
            t = jnp.zeros((X, C), f32)
            for g in range(F):
                t = jnp.where(count - 2 + f == frame_of[g], v[g], t)
            got.append(t)
        return jnp.concatenate(got, axis=0).astype(bf16)

    def put_tail_cols(tails, dst):
        v = tails[...].astype(f32)
        more = dst.shape[1] - v.shape[0]
        for f in range(2):
            c = edge(v, f * X)
            if more:
                c = jnp.concatenate([c, jnp.zeros((more, C), f32)], axis=0)
            dst[f] = c.astype(bf16)

    def tiles(b):
        zero = jnp.zeros((X, C), f32)
        front = jnp.concatenate([zero, b[2 * (H - 2)], zero, b[2 * (H - 1)]], axis=0)
        return jnp.concatenate([front, b.reshape(S, C)], axis=0).astype(bf16)

    def center(yy, v):
        t = tiles(v)
        lo[1, yy] = t[:, :LANES]
        high = t[:, LANES:]
        after = jnp.concatenate([high[T:], jnp.zeros((T, C - LANES), bf16)], axis=0)
        hc[yy] = jnp.concatenate([high, after], axis=1)

    def beside(v, col):
        index = lax.broadcasted_iota(jnp.int32, v.shape, 1)
        none = jnp.zeros(col.shape, f32)
        lcol = jnp.where(left_core, none, col)
        rcol = jnp.where(left_core, col, none)
        left = jnp.where(index == 0, jnp.broadcast_to(lcol[:, None, :], v.shape), pltpu.roll(v, 1, 1))
        right = jnp.where(index == X - 1, jnp.broadcast_to(rcol[:, None, :], v.shape), pltpu.roll(v, X - 1, 1))
        return left, right

    def sides(yy, v, col):
        left, right = beside(v, col)
        tl, tr = tiles(left), tiles(right)
        lo[0, yy] = tl[:, :LANES]
        lo[2, yy] = tr[:, :LANES]
        hs[yy] = jnp.concatenate([tl[:, LANES:], tr[:, LANES:]], axis=1)

    def grouped(ref, index):
        return jnp.concatenate([ref[(t,) + index].astype(f32)[None] for t in frame_of], axis=0)

    def as_groups(ref, y):
        return ref[y].astype(f32).reshape(F, X, C)

    def conv(y0, n, wl, wc, ws):
        def take(ref, i, a):
            return ref[pl.ds(y0 + i, n), pl.ds(a * T, S)].reshape(n * S, LANES)

        lhs, rhs = [], []
        for i in range(3):
            lhs += [take(lo.at[j], i, a) for a in range(3) for j in range(3)]
            lhs += [take(hc, i, 0), take(hc, i, 2)] + [take(hs, i, a) for a in range(3)]
            rhs += [wl[a, i].reshape(3 * LANES, C) for a in range(3)]
            rhs += [wc[0, i], wc[1, i]] + [ws[a, i] for a in range(3)]
        acc[pl.ds(y0 * S, n * S)] = jnp.dot(
            jnp.concatenate(lhs, axis=1), jnp.concatenate(rhs, axis=0), preferred_element_type=f32
        )

    def before(first, n, wl, wc, ws):
        carry[...] = jnp.zeros(carry.shape, f32)
        carry_col[...] = jnp.zeros(carry_col.shape, f32)
        for k in range(n_t - 1):
            @pl.when(me_t > k)
            def _(k=k):
                for i in (8, 0, 1) if first else (6, 7):
                    far(k, k, i).wait_recv()
                if first:
                    @pl.when(has[0])
                    def _():
                        for i in (4, 5):
                            far(k, k, i, -1).wait_recv()

                    @pl.when(has[1])
                    def _():
                        for i in (2, 3):
                            far(k, k, i, -1).wait_recv()

                total = cnt_in[k]

                def merge(total, early0, early1, late0, late1):
                    both, some = total > 1.5, total > 0.5
                    return (
                        jnp.where(both, late0, jnp.where(some, early1, early0)),
                        jnp.where(some, late1, early1),
                    )

                for at in range(n + 2):
                    late = (tail_in1 if first else tail_in2)[k, at].astype(f32)
                    got = merge(total, carry[at, :X], carry[at, X:], late[:X], late[X:])
                    carry[at] = jnp.concatenate(got, axis=0)
                cols = (tailc_in1.at[k], tailhc_in.at[k, 0], tailhc_in.at[k, 1]) if first else (tailc_in2.at[k],)
                for d, ref in enumerate(cols):
                    late = ref[...].astype(f32)
                    there = pl.ds(0, late.shape[1])
                    got = merge(total[:1], carry_col[d, 0, there], carry_col[d, 1, there], late[0], late[1])
                    carry_col[d, 0, there] = got[0]
                    carry_col[d, 1, there] = got[1]

        zero = jnp.zeros((X, C), f32)
        for yy in range(n + 2):
            at, d, y = yy, 0, yy
            if first:
                if yy < 2:
                    at, d, y = R + yy, 1, R - 2 + yy
                elif yy < R + 2:
                    at, d, y = yy - 2, 0, yy - 2
                else:
                    d, y = 2, yy - R - 2
            col = jnp.concatenate([carry_col[d, f, y : y + 1] for f in range(2)], axis=0)
            v = carry[at].reshape(2, X, C)
            left, right = beside(v, col)
            made = []
            for j, b in enumerate((left, v, right)):
                t = jnp.concatenate([b[0], b[1], b[1], zero], axis=0).astype(bf16)
                clo[j, yy] = t[:, :LANES]
                made.append(t[:, LANES:])
            chs[yy] = jnp.concatenate([made[0], made[2]], axis=1)
            chc[yy] = jnp.concatenate([made[1][:T], made[1][T:]], axis=1)
        lhs, rhs = [], []
        for i in range(3):
            for a in range(2):
                for j in range(3):
                    lhs.append(clo[j, pl.ds(i, n), pl.ds(a * T, T)].reshape(n * T, LANES))
                lhs.append(chs[pl.ds(i, n), pl.ds(a * T, T)].reshape(n * T, LANES))
                rhs += [wl[a, i].reshape(3 * LANES, C), ws[a, i]]
            lhs.append(chc[pl.ds(i, n)].reshape(n * T, LANES))
            rhs.append(wc[0, i])
        part = jnp.dot(jnp.concatenate(lhs, axis=1), jnp.concatenate(rhs, axis=0), preferred_element_type=f32)
        for y in range(n):
            for f in range(2):
                acc[pl.ds(y * S + f * T, X)] += part[y * T + f * X : y * T + (f + 1) * X]

    pl.semaphore_wait(barrier, expected)
    tell_lower(over)

    @pl.when(has[0])
    def _():
        tell(up.at[0], me_t, -1, False)
        tell(up.at[1], me_t, -1, True)
        row_copy(0).start()

    load_feat.wait()
    load_g1.wait()

    def keep_first(y):
        v = silu_norm(grouped(feat, (y,)), g1[...].reshape(1, 1, C))
        v = jnp.where(live, v, 0.0)
        rows1[y] = v.reshape(S, C).astype(bf16)
        col_out1[y] = edge(v).astype(bf16)
        if n_t > 1:
            tail1[y] = tail_of(v)
        center(y + 2, v)

    ends = sorted({0, 1, R - 2, R - 1})
    for y in ends:
        keep_first(y)

    @pl.when(has[0])
    def _():
        corner_copy(0).start()

    for y in range(R):
        if y not in ends:
            keep_first(y)
    col_copy(True).start()

    @pl.when(has[1])
    def _():
        pl.semaphore_wait(up.at[0], 1)
        pl.semaphore_wait(up.at[1], 1)
        row_copy(1).start()
        corner_copy(1).start()
        tell_lower(over_up)

    if n_t > 1:
        put_tail_cols(tail1, tailc1)

        def tails_first(k):
            pl.semaphore_wait(over.at[k], 1)
            for i in (8, 0, 1):
                far(k, me_t, i).start()
            aside(lambda i: far(k, me_t, i).start(), 0)

            @pl.when(has[1])
            def _():
                pl.semaphore_wait(over_up.at[k], 1)

            aside(lambda i: far(k, me_t, i).start(), 1)

        later(tails_first)
    col_copy(True).wait_recv()
    for y in range(R):
        sides(y + 2, as_groups(rows1, y), col_in1[y + 2].astype(f32))
    for c in load_w1:
        c.wait()
    half = (R - 2) // 2
    conv(2, half, wl1, wc1, ws1)
    conv(2 + half, R - 2 - half, wl1, wc1, ws1)
    for side in range(2):
        @pl.when(has[side])
        def _(side=side):
            row_copy(1 - side, -1).wait_recv()
            corner_copy(1 - side, -1).wait_recv()
    for side in range(2):
        for r in range(2):
            v = silu_norm(grouped(raw_in.at[side], (r,)), g1[...].reshape(1, 1, C))
            v = jnp.where(live, v, 0.0)
            yy = side * (R + 2) + r
            v = v.astype(bf16).astype(f32)
            center(yy, v)
            sides(yy, v, col_in1[yy].astype(f32))
    conv(0, 2, wl1, wc1, ws1)
    conv(R, 2, wl1, wc1, ws1)
    if n_t > 1:
        @pl.when(me_t > 0)
        def _():
            before(True, R + 2, wl1, wc1, ws1)

    for c in load_rest:
        c.wait()
    for h in range(R + 2):
        v = silu_norm(acc[pl.ds(h * S, S)] + b1[...], g2[...]).reshape(F, X, C)
        v = jnp.where(live, v, 0.0)
        if h in (0, R + 1):
            v = jnp.where(has[min(h, 1)], v, 0.0)
        rows2[h] = v.reshape(S, C).astype(bf16)
        col_out2[h] = edge(v).astype(bf16)
        if n_t > 1:
            tail2[h] = tail_of(v)
        center(h, v)
    col_copy(False).start()
    if n_t > 1:
        put_tail_cols(tail2, tailc2)


        def tails_second(k):
            for i in (6, 7):
                far(k, me_t, i).start()

        later(tails_second)
    col_copy(False).wait_recv()
    for h in range(R + 2):
        sides(h, as_groups(rows2, h), col_in2[h].astype(f32))
    for c in load_w2:
        c.wait()
    conv(0, R, wl2, wc2, ws2)
    if n_t > 1:
        @pl.when(me_t > 0)
        def _():
            before(False, R, wl2, wc2, ws2)

    for y in range(R):
        result = acc[pl.ds(y * S, S)] + b2[...]
        for g in range(F):
            t = frame_of[g]
            value = feat[t, y].astype(f32) + result[g * X : (g + 1) * X]
            out[t, y] = jnp.where(live[g], value, 0.0).astype(bf16)

    col_copy(True).wait_send()
    col_copy(False).wait_send()
    for side in range(2):
        @pl.when(has[side])
        def _(side=side):
            row_copy(side).wait_send()
            corner_copy(side).wait_send()

    def sent(k):
        for i in (8, 0, 1, 6, 7):
            far(k, me_t, i).wait_send()
        for side in range(2):
            aside(lambda i: far(k, me_t, i).wait_send(), side)

    later(sent)


def shards(sizes, features, frame_counts, gain_first, conv_first, bias_first, gain_second, conv_second, bias_second):
    F, R, X, C = features.shape
    n_t, n_z, n_w = sizes
    assert n_w == 2 and F % 2 == 0 and F >= 4 and X == 8 and 2 * (C - LANES) == LANES and R >= 4
    H = F // 2
    S, T = F * X, 2 * X
    wide = -(-(R + 2) // 16) * 16
    dma = pltpu.SemaphoreType.DMA
    V = pltpu.VMEM
    weights = [V((3, 3, 3, LANES, C), bf16), V((2, 3, LANES, C), bf16), V((3, 3, LANES, C), bf16)]
    scratch = [
        V(features.shape, bf16),
        V((1, C), f32),
        V((1, C), f32),
        V((1, C), f32),
        V((1, C), f32),
        *weights,
        *weights,
        dma((17,)),
        V((3, R + 4, (H + 2) * T, LANES), bf16),
        V((R + 4, (H + 2) * T, LANES), bf16),
        V((R + 4, (H + 2) * T, LANES), bf16),
        V(((R + 2) * S, C), f32),
        V((3, R + 4, 2 * T, LANES), bf16),
        V((R + 4, T, LANES), bf16),
        V((R + 4, 2 * T, LANES), bf16),
        V((X, C), f32),
        V((n_t, X, C), f32),
        V((R + 4, T, C), f32),
        V((3, 2, max(R, wide), C), f32),
        V((2, F, 2, X, C), bf16),
        V((R, S, C), bf16),
        V((R, F, C), bf16),
        V((R + 4, F, C), bf16),
        V((R, T, C), bf16),
        V((2, R, C), bf16),
        V((n_t, R + 4, T, C), bf16),
        V((n_t, 2, R, C), bf16),
        V((n_t, 2, 2, R, C), bf16),
        V((R + 2, S, C), bf16),
        V((R + 2, F, C), bf16),
        V((R + 2, F, C), bf16),
        V((R + 2, T, C), bf16),
        V((2, wide, C), bf16),
        V((n_t, R + 2, T, C), bf16),
        V((n_t, 2, wide, C), bf16),
        dma((6,)),
        dma((6,)),
        dma((n_t, 9)),
        dma((n_t, 9)),
        pltpu.SemaphoreType.REGULAR((2,)),
        pltpu.SemaphoreType.REGULAR((n_t,)),
        pltpu.SemaphoreType.REGULAR((n_t,)),
    ]
    return pl.pallas_call(
        functools.partial(kernel, sizes),
        out_shape=pltpu.VMEM(features.shape, features.dtype),
        in_specs=[pl.BlockSpec(memory_space=pltpu.SMEM)] + [pl.BlockSpec(memory_space=pltpu.HBM)] * 7,
        out_specs=pl.BlockSpec(memory_space=pltpu.VMEM),
        scratch_shapes=scratch,
        compiler_params=pltpu.CompilerParams(
            collective_id=0, has_side_effects=True, vmem_limit_bytes=58 << 20
        ),
    )(
        frame_counts,
        features,
        gain_first.reshape(1, C),
        conv_first,
        bias_first.reshape(1, C),
        gain_second.reshape(1, C),
        conv_second,
        bias_second.reshape(1, C),
    )


def solution(mesh):
    sizes = (mesh.shape["tchunk"], mesh.shape["ha"], mesh.shape["wa"])
    spec = P(("grp", "tchunk"), "ha", "wa", None)
    return jax.shard_map(
        functools.partial(shards, sizes),
        mesh=mesh,
        in_specs=(spec, P(("grp", "tchunk")), P(), P(), P(), P(), P(), P()),
        out_specs=spec,
        check_vma=False,
    )
```

time: 15.5 us -> 13.7 us (0.88)
  Pallas kernels: 13.9 us -> 12.2 us
    pallas_call x1, Pallas kernels: 13.9 us -> 12.2 us  [shards(): pl.pallas_call(functools.partial(kernel, sizes), out_shape=pltpu.VMEM(fea...]
where the time goes in v2:
time: 13.7 us; the launch traced here: 13.6 us
  Pallas kernels  12.2 us (89%)
  local copies, waits for them, and re-layouts  0.71 us (5%)
  between operations  0.66 us (5%)
    pallas_call x1, Pallas kernels, shards(): pl.pallas_call(functools.partial(kernel, sizes), out_shape=pltpu.VMEM(fea...  12.2 us
    unnamed x1, local copies, waits for them, and re-layouts  0.71 us

profile of v2, /device:TPU:15, one launch (start us, length us, event | category | flops | bytes accessed | tf_op | source)
XLA Modules:
  0.0 13.6 jit_solution(18115315828996521250)
XLA Ops:
  0.7 12.2 %shard_map.82 = bf16[8,8,8,192]{3,2,1,0:T(8,128)(2,1)S(1)} custom-call(s32[1]{0:T(128)S(6)} %copy.11.refs_0_, bf16[8,8,8,192]{3,2,1,0:T(8,128)(2,1)} %refs_1_.1, f32[1,192]{1,0:T(1,128)} %bitcast.4, bf16[3,3,3,192,192]{4,3,2,1,0:T(8,128)(2,1)} %refs_3_.1, f32[1,192]{1,0:T(1,128)} %bitcast.5, f32[1,192]{1,0:T(1,128)} %bitcast.6, ...), custom_call_target="tpu_custom_call" | custom-call | tf_op jit(solution)/shard_map/pallas_call | solution.py:500
  12.8 0.7 %copy.10 = bf16[8,8,8,192]{3,2,1,0:T(8,128)(2,1)} copy(bf16[8,8,8,192]{3,2,1,0:T(8,128)(2,1)S(1)} %shard_map.82) | data formatting | bytes 393216

commit v3 on v2

--- a/solution.py
+++ b/solution.py
@@ -22,10 +22,10 @@
     placed, out, scratch = refs[:8], refs[8], refs[9:]
     n_t, n_z, n_w = sizes
     cnt_ref, feat_hbm, g1_hbm, w1_hbm, b1_hbm, g2_hbm, w2_hbm, b2_hbm = placed
-    (feat, g1, b1, g2, b2, wl1, wc1, ws1, wl2, wc2, ws2, lsem, lo, hc, hs, acc,
+    (feat, g1, b1, g2, b2, wl1, wc1, ws1, wl2, wc2, ws2, lsem, lo1, hc1, hs1, lo2, hc2, hs2, acc,
      clo, chc, chs, cnt_own, cnt_in, carry, carry_col,
      raw_in, rows1, col_out1, col_in1, tail1, tailc1, tail_in1, tailc_in1, tailhc_in,
-     rows2, col_out2, col_in2, tail2, tailc2, tail_in2, tailc_in2,
+     rows2, col_out2, col_in2, tail2, tailc2, taile2, tail_in2, tailc_in2, taile_in2,
      nsend, nrecv, fsend, frecv, up, over, over_up) = scratch
     F, R, X, C = feat.shape
     H = F // 2
@@ -123,9 +123,11 @@
             (tailc1, tailhc_in.at[slot, 1], -1, True),
             (tail1.at[pl.ds(R - 2, 2)], tail_in1.at[slot, pl.ds(R, 2)], 1, False),
             (tailc1, tailhc_in.at[slot, 0], 1, True),
-            (tail2, tail_in2.at[slot], 0, False),
+            (tail2.at[pl.ds(0, R - 2)], tail_in2.at[slot, pl.ds(0, R - 2)], 0, False),
             (tailc2, tailc_in2.at[slot], 0, True),
             (cnt_own, cnt_in.at[slot], 0, False),
+            (tail2.at[pl.ds(R - 2, 4)], tail_in2.at[slot, pl.ds(R - 2, 4)], 0, False),
+            (taile2, taile_in2.at[slot], 0, True),
         )[i]
         return remote(src, dst, fsend.at[k, i], frecv.at[slot, i], device(k, way * dz, flip))
 
@@ -169,6 +171,9 @@
             got.append(t)
         return jnp.concatenate(got, axis=0).astype(bf16)
 
+    def slot_of(h):
+        return h - 2 if 2 <= h < R else R - 2 + h if h < 2 else h
+
     def put_tail_cols(tails, dst):
         v = tails[...].astype(f32)
         more = dst.shape[1] - v.shape[0]
@@ -183,7 +188,10 @@
         front = jnp.concatenate([zero, b[2 * (H - 2)], zero, b[2 * (H - 1)]], axis=0)
         return jnp.concatenate([front, b.reshape(S, C)], axis=0).astype(bf16)
 
-    def center(yy, v):
+    tiles1, tiles2 = (lo1, hc1, hs1), (lo2, hc2, hs2)
+
+    def center(into, yy, v):
+        lo, hc, _ = into
         t = tiles(v)
         lo[1, yy] = t[:, :LANES]
         high = t[:, LANES:]
@@ -199,7 +207,8 @@
         right = jnp.where(index == X - 1, jnp.broadcast_to(rcol[:, None, :], v.shape), pltpu.roll(v, X - 1, 1))
         return left, right
 
-    def sides(yy, v, col):
+    def sides(into, yy, v, col):
+        lo, _, hs = into
         left, right = beside(v, col)
         tl, tr = tiles(left), tiles(right)
         lo[0, yy] = tl[:, :LANES]
@@ -212,19 +221,25 @@
     def as_groups(ref, y):
         return ref[y].astype(f32).reshape(F, X, C)
 
-    def conv(y0, n, wl, wc, ws):
+    def conv(of, y0, n, wl, wc, ws, part=None):
+        lo, hc, hs = of
+
         def take(ref, i, a):
             return ref[pl.ds(y0 + i, n), pl.ds(a * T, S)].reshape(n * S, LANES)
 
         lhs, rhs = [], []
         for i in range(3):
-            lhs += [take(lo.at[j], i, a) for a in range(3) for j in range(3)]
-            lhs += [take(hc, i, 0), take(hc, i, 2)] + [take(hs, i, a) for a in range(3)]
-            rhs += [wl[a, i].reshape(3 * LANES, C) for a in range(3)]
-            rhs += [wc[0, i], wc[1, i]] + [ws[a, i] for a in range(3)]
-        acc[pl.ds(y0 * S, n * S)] = jnp.dot(
-            jnp.concatenate(lhs, axis=1), jnp.concatenate(rhs, axis=0), preferred_element_type=f32
-        )
+            if part != "sides":
+                lhs += [take(lo.at[1], i, a) for a in range(3)] + [take(hc, i, 0), take(hc, i, 2)]
+                rhs += [wl[a, i, 1] for a in range(3)] + [wc[0, i], wc[1, i]]
+            if part != "center":
+                lhs += [take(lo.at[j], i, a) for a in range(3) for j in (0, 2)] + [take(hs, i, a) for a in range(3)]
+                rhs += [wl[a, i, j] for a in range(3) for j in (0, 2)] + [ws[a, i] for a in range(3)]
+        got = jnp.dot(jnp.concatenate(lhs, axis=1), jnp.concatenate(rhs, axis=0), preferred_element_type=f32)
+        if part == "sides":
+            acc[pl.ds(y0 * S, n * S)] += got
+        else:
+            acc[pl.ds(y0 * S, n * S)] = got
 
     def before(first, n, wl, wc, ws):
         carry[...] = jnp.zeros(carry.shape, f32)
@@ -232,7 +247,7 @@
         for k in range(n_t - 1):
             @pl.when(me_t > k)
             def _(k=k):
-                for i in (8, 0, 1) if first else (6, 7):
+                for i in (8, 0, 1) if first else (6, 7, 9, 10):
                     far(k, k, i).wait_recv()
                 if first:
                     @pl.when(has[0])
@@ -258,7 +273,7 @@
                     late = (tail_in1 if first else tail_in2)[k, at].astype(f32)
                     got = merge(total, carry[at, :X], carry[at, X:], late[:X], late[X:])
                     carry[at] = jnp.concatenate(got, axis=0)
-                cols = (tailc_in1.at[k], tailhc_in.at[k, 0], tailhc_in.at[k, 1]) if first else (tailc_in2.at[k],)
+                cols = (tailc_in1.at[k], tailhc_in.at[k, 0], tailhc_in.at[k, 1]) if first else (tailc_in2.at[k], taile_in2.at[k])
                 for d, ref in enumerate(cols):
                     late = ref[...].astype(f32)
                     there = pl.ds(0, late.shape[1])
@@ -268,7 +283,8 @@
 
         zero = jnp.zeros((X, C), f32)
         for yy in range(n + 2):
-            at, d, y = yy, 0, yy
+            at = slot_of(yy)
+            d, y = (0, at) if at < R - 2 else (1, at - R + 2)
             if first:
                 if yy < 2:
                     at, d, y = R + yy, 1, R - 2 + yy
@@ -319,7 +335,7 @@
         col_out1[y] = edge(v).astype(bf16)
         if n_t > 1:
             tail1[y] = tail_of(v)
-        center(y + 2, v)
+        center(tiles1, y + 2, v)
 
     ends = sorted({0, 1, R - 2, R - 1})
     for y in ends:
@@ -360,12 +376,44 @@
         later(tails_first)
     col_copy(True).wait_recv()
     for y in range(R):
-        sides(y + 2, as_groups(rows1, y), col_in1[y + 2].astype(f32))
+        sides(tiles1, y + 2, as_groups(rows1, y), col_in1[y + 2].astype(f32))
     for c in load_w1:
         c.wait()
     half = (R - 2) // 2
-    conv(2, half, wl1, wc1, ws1)
-    conv(2 + half, R - 2 - half, wl1, wc1, ws1)
+    conv(tiles1, 2, half, wl1, wc1, ws1)
+    conv(tiles1, 2 + half, R - 2 - half, wl1, wc1, ws1)
+    for c in load_rest:
+        c.wait()
+
+    def second(h, groups):
+        v = silu_norm(acc[pl.ds(h * S, groups * X)] + b1[...], g2[...]).reshape(groups, X, C)
+        v = jnp.where(live[:groups], v, 0.0)
+        if h in (0, R + 1):
+            v = jnp.where(has[min(h, 1)], v, 0.0)
+        rows2[h, : groups * X] = v.reshape(groups * X, C).astype(bf16)
+        return v
+
+    def keep_second(h, v, tails=n_t > 1):
+        if tails:
+            tail2[slot_of(h)] = tail_of(v)
+        col_out2[h] = edge(v).astype(bf16)
+        center(tiles2, h, v)
+
+    def tails_second(which):
+        def act(k):
+            for i in which:
+                far(k, me_t, i).start()
+
+        return act
+
+    for h in range(2, R):
+        keep_second(h, second(h, F))
+    if n_t > 1:
+        @pl.when(me_t == 0)
+        def _():
+            put_tail_cols(tail2.at[pl.ds(0, R - 2)], tailc2)
+            later(tails_second((6, 7)))
+
     for side in range(2):
         @pl.when(has[side])
         def _(side=side):
@@ -377,43 +425,41 @@
             v = jnp.where(live, v, 0.0)
             yy = side * (R + 2) + r
             v = v.astype(bf16).astype(f32)
-            center(yy, v)
-            sides(yy, v, col_in1[yy].astype(f32))
-    conv(0, 2, wl1, wc1, ws1)
-    conv(R, 2, wl1, wc1, ws1)
+            center(tiles1, yy, v)
+            sides(tiles1, yy, v, col_in1[yy].astype(f32))
+    conv(tiles1, 0, 2, wl1, wc1, ws1)
+    conv(tiles1, R, 2, wl1, wc1, ws1)
+    for h in (0, 1, R, R + 1):
+        keep_second(h, second(h, F))
     if n_t > 1:
+        @pl.when(me_t == 0)
+        def _():
+            put_tail_cols(tail2.at[pl.ds(R - 2, 4)], taile2)
+            later(tails_second((9, 10)))
+
         @pl.when(me_t > 0)
         def _():
             before(True, R + 2, wl1, wc1, ws1)
-
-    for c in load_rest:
+            for h in range(R + 2):
+                v = second(h, 4)
+                rest = rows2[h, 4 * X :].astype(f32).reshape(F - 4, X, C)
+                keep_second(h, jnp.concatenate([v, rest], axis=0), n_t > 2)
+            if n_t > 2:
+                put_tail_cols(tail2.at[pl.ds(0, R - 2)], tailc2)
+                put_tail_cols(tail2.at[pl.ds(R - 2, 4)], taile2)
+                later(tails_second((6, 7, 9, 10)))
+
+    col_copy(False).start()
+
+    for c in load_w2:
         c.wait()
-    for h in range(R + 2):
-        v = silu_norm(acc[pl.ds(h * S, S)] + b1[...], g2[...]).reshape(F, X, C)
-        v = jnp.where(live, v, 0.0)
-        if h in (0, R + 1):
-            v = jnp.where(has[min(h, 1)], v, 0.0)
-        rows2[h] = v.reshape(S, C).astype(bf16)
-        col_out2[h] = edge(v).astype(bf16)
-        if n_t > 1:
-            tail2[h] = tail_of(v)
-        center(h, v)
-    col_copy(False).start()
-    if n_t > 1:
-        put_tail_cols(tail2, tailc2)
-
-
-        def tails_second(k):
-            for i in (6, 7):
-                far(k, me_t, i).start()
-
-        later(tails_second)
+    for y in (0, R // 2):
+        conv(tiles2, y, R // 2 if y == 0 else R - R // 2, wl2, wc2, ws2, "center")
     col_copy(False).wait_recv()
     for h in range(R + 2):
-        sides(h, as_groups(rows2, h), col_in2[h].astype(f32))
-    for c in load_w2:
-        c.wait()
-    conv(0, R, wl2, wc2, ws2)
+        sides(tiles2, h, as_groups(rows2, h), col_in2[h].astype(f32))
+    for y in (0, R // 2):
+        conv(tiles2, y, R // 2 if y == 0 else R - R // 2, wl2, wc2, ws2, "sides")
     if n_t > 1:
         @pl.when(me_t > 0)
         def _():
@@ -435,7 +481,7 @@
             corner_copy(side).wait_send()
 
     def sent(k):
-        for i in (8, 0, 1, 6, 7):
+        for i in (8, 0, 1, 6, 7, 9, 10):
             far(k, me_t, i).wait_send()
         for side in range(2):
             aside(lambda i: far(k, me_t, i).wait_send(), side)
@@ -449,7 +495,7 @@
     assert n_w == 2 and F % 2 == 0 and F >= 4 and X == 8 and 2 * (C - LANES) == LANES and R >= 4
     H = F // 2
     S, T = F * X, 2 * X
-    wide = -(-(R + 2) // 16) * 16
+    inner = -(-(R - 2) // 8) * 8
     dma = pltpu.SemaphoreType.DMA
     V = pltpu.VMEM
     weights = [V((3, 3, 3, LANES, C), bf16), V((2, 3, LANES, C), bf16), V((3, 3, LANES, C), bf16)]
@@ -465,6 +511,9 @@
         V((3, R + 4, (H + 2) * T, LANES), bf16),
         V((R + 4, (H + 2) * T, LANES), bf16),
         V((R + 4, (H + 2) * T, LANES), bf16),
+        V((3, R + 2, (H + 2) * T, LANES), bf16),
+        V((R + 2, (H + 2) * T, LANES), bf16),
+        V((R + 2, (H + 2) * T, LANES), bf16),
         V(((R + 2) * S, C), f32),
         V((3, R + 4, 2 * T, LANES), bf16),
         V((R + 4, T, LANES), bf16),
@@ -472,7 +521,7 @@
         V((X, C), f32),
         V((n_t, X, C), f32),
         V((R + 4, T, C), f32),
-        V((3, 2, max(R, wide), C), f32),
+        V((3, 2, max(R, inner, 8), C), f32),
         V((2, F, 2, X, C), bf16),
         V((R, S, C), bf16),
         V((R, F, C), bf16),
@@ -486,13 +535,15 @@
         V((R + 2, F, C), bf16),
         V((R + 2, F, C), bf16),
         V((R + 2, T, C), bf16),
-        V((2, wide, C), bf16),
+        V((2, inner, C), bf16),
+        V((2, 8, C), bf16),
         V((n_t, R + 2, T, C), bf16),
-        V((n_t, 2, wide, C), bf16),
+        V((n_t, 2, inner, C), bf16),
+        V((n_t, 2, 8, C), bf16),
         dma((6,)),
         dma((6,)),
-        dma((n_t, 9)),
-        dma((n_t, 9)),
+        dma((n_t, 11)),
+        dma((n_t, 11)),
         pltpu.SemaphoreType.REGULAR((2,)),
         pltpu.SemaphoreType.REGULAR((n_t,)),
         pltpu.SemaphoreType.REGULAR((n_t,)),

time: 13.7 us -> 12.8 us (0.934)
  Pallas kernels: 12.2 us -> 11.3 us
    pallas_call x1, Pallas kernels: 12.2 us -> 11.3 us  [shards(): pl.pallas_call(functools.partial(kernel, sizes), out_shape=pltpu.VMEM(fea...]
where the time goes in v3:
time: 12.8 us; the launch traced here: 12.7 us
  Pallas kernels  11.3 us (88%)
  local copies, waits for them, and re-layouts  0.71 us (6%)
  between operations  0.66 us (5%)
    pallas_call x1, Pallas kernels, shards(): pl.pallas_call(functools.partial(kernel, sizes), out_shape=pltpu.VMEM(fea...  11.3 us
    unnamed x1, local copies, waits for them, and re-layouts  0.71 us

profile of v3, /device:TPU:15, one launch (start us, length us, event | category | flops | bytes accessed | tf_op | source)
XLA Modules:
  0.0 12.7 jit_solution(17507131383247905369)
XLA Ops:
  0.7 11.3 %shard_map.82 = bf16[8,8,8,192]{3,2,1,0:T(8,128)(2,1)S(1)} custom-call(s32[1]{0:T(128)S(6)} %copy.11.refs_0_, bf16[8,8,8,192]{3,2,1,0:T(8,128)(2,1)} %refs_1_.1, f32[1,192]{1,0:T(1,128)} %bitcast.4, bf16[3,3,3,192,192]{4,3,2,1,0:T(8,128)(2,1)} %refs_3_.1, f32[1,192]{1,0:T(1,128)} %bitcast.5, f32[1,192]{1,0:T(1,128)} %bitcast.6, ...), custom_call_target="tpu_custom_call" | custom-call | tf_op jit(solution)/shard_map/pallas_call | solution.py:551
  12.0 0.7 %copy.10 = bf16[8,8,8,192]{3,2,1,0:T(8,128)(2,1)} copy(bf16[8,8,8,192]{3,2,1,0:T(8,128)(2,1)S(1)} %shard_map.82) | data formatting | bytes 393216

commit v4 on v3

--- a/solution.py
+++ b/solution.py
@@ -221,14 +221,14 @@
     def as_groups(ref, y):
         return ref[y].astype(f32).reshape(F, X, C)
 
-    def conv(of, y0, n, wl, wc, ws, part=None):
+    def conv(of, y0, n, wl, wc, ws, part=None, taps=(0, 1, 2), add=False):
         lo, hc, hs = of
 
         def take(ref, i, a):
             return ref[pl.ds(y0 + i, n), pl.ds(a * T, S)].reshape(n * S, LANES)
 
         lhs, rhs = [], []
-        for i in range(3):
+        for i in taps:
             if part != "sides":
                 lhs += [take(lo.at[1], i, a) for a in range(3)] + [take(hc, i, 0), take(hc, i, 2)]
                 rhs += [wl[a, i, 1] for a in range(3)] + [wc[0, i], wc[1, i]]
@@ -236,7 +236,7 @@
                 lhs += [take(lo.at[j], i, a) for a in range(3) for j in (0, 2)] + [take(hs, i, a) for a in range(3)]
                 rhs += [wl[a, i, j] for a in range(3) for j in (0, 2)] + [ws[a, i] for a in range(3)]
         got = jnp.dot(jnp.concatenate(lhs, axis=1), jnp.concatenate(rhs, axis=0), preferred_element_type=f32)
-        if part == "sides":
+        if part == "sides" or add:
             acc[pl.ds(y0 * S, n * S)] += got
         else:
             acc[pl.ds(y0 * S, n * S)] = got
@@ -333,8 +333,6 @@
         v = jnp.where(live, v, 0.0)
         rows1[y] = v.reshape(S, C).astype(bf16)
         col_out1[y] = edge(v).astype(bf16)
-        if n_t > 1:
-            tail1[y] = tail_of(v)
         center(tiles1, y + 2, v)
 
     ends = sorted({0, 1, R - 2, R - 1})
@@ -353,13 +351,17 @@
     @pl.when(has[1])
     def _():
         pl.semaphore_wait(up.at[0], 1)
+        row_copy(1).start()
         pl.semaphore_wait(up.at[1], 1)
-        row_copy(1).start()
         corner_copy(1).start()
         tell_lower(over_up)
 
     if n_t > 1:
-        put_tail_cols(tail1, tailc1)
+        @pl.when(me_t < n_t - 1)
+        def _():
+            for y in range(R):
+                tail1[y] = tail_of(as_groups(rows1, y))
+            put_tail_cols(tail1, tailc1)
 
         def tails_first(k):
             pl.semaphore_wait(over.at[k], 1)
@@ -367,21 +369,34 @@
                 far(k, me_t, i).start()
             aside(lambda i: far(k, me_t, i).start(), 0)
 
+        def tails_up(k):
             @pl.when(has[1])
             def _():
                 pl.semaphore_wait(over_up.at[k], 1)
-
-            aside(lambda i: far(k, me_t, i).start(), 1)
+                for i in (4, 5):
+                    far(k, me_t, i).start()
 
         later(tails_first)
     col_copy(True).wait_recv()
     for y in range(R):
         sides(tiles1, y + 2, as_groups(rows1, y), col_in1[y + 2].astype(f32))
+    if n_t > 1:
+        @pl.when(me_z > 0)
+        def _():
+            later(tails_up)
+
     for c in load_w1:
         c.wait()
     half = (R - 2) // 2
     conv(tiles1, 2, half, wl1, wc1, ws1)
     conv(tiles1, 2 + half, R - 2 - half, wl1, wc1, ws1)
+    conv(tiles1, 0, 2, wl1, wc1, ws1, taps=(2,))
+    conv(tiles1, R, 2, wl1, wc1, ws1, taps=(0,))
+    if n_t > 1:
+        @pl.when(me_z == 0)
+        def _():
+            later(tails_up)
+
     for c in load_rest:
         c.wait()
 
@@ -393,11 +408,14 @@
         rows2[h, : groups * X] = v.reshape(groups * X, C).astype(bf16)
         return v
 
-    def keep_second(h, v, tails=n_t > 1):
-        if tails:
-            tail2[slot_of(h)] = tail_of(v)
+    def keep_second(h, v):
         col_out2[h] = edge(v).astype(bf16)
         center(tiles2, h, v)
+
+    def put_tails(rows, at, n, dst):
+        for h in rows:
+            tail2[slot_of(h)] = tail_of(as_groups(rows2, h))
+        put_tail_cols(tail2.at[pl.ds(at, n)], dst)
 
     def tails_second(which):
         def act(k):
@@ -411,7 +429,7 @@
     if n_t > 1:
         @pl.when(me_t == 0)
         def _():
-            put_tail_cols(tail2.at[pl.ds(0, R - 2)], tailc2)
+            put_tails(range(2, R), 0, R - 2, tailc2)
             later(tails_second((6, 7)))
 
     for side in range(2):
@@ -427,27 +445,40 @@
             v = v.astype(bf16).astype(f32)
             center(tiles1, yy, v)
             sides(tiles1, yy, v, col_in1[yy].astype(f32))
-    conv(tiles1, 0, 2, wl1, wc1, ws1)
-    conv(tiles1, R, 2, wl1, wc1, ws1)
-    for h in (0, 1, R, R + 1):
-        keep_second(h, second(h, F))
+    conv(tiles1, 0, 2, wl1, wc1, ws1, taps=(0, 1), add=True)
+    conv(tiles1, R, 2, wl1, wc1, ws1, taps=(1, 2), add=True)
+    ends = (0, 1, R, R + 1)
+
+    @pl.when(me_t == 0)
+    def _():
+        for h in ends:
+            keep_second(h, second(h, F))
+        if n_t > 1:
+            put_tails(ends, R - 2, 4, taile2)
+            later(tails_second((9, 10)))
+
     if n_t > 1:
-        @pl.when(me_t == 0)
-        def _():
-            put_tail_cols(tail2.at[pl.ds(R - 2, 4)], taile2)
-            later(tails_second((9, 10)))
-
         @pl.when(me_t > 0)
         def _():
             before(True, R + 2, wl1, wc1, ws1)
-            for h in range(R + 2):
+            for h in ends:
+                keep_second(h, second(h, F))
+            for h in range(2, R):
                 v = second(h, 4)
                 rest = rows2[h, 4 * X :].astype(f32).reshape(F - 4, X, C)
-                keep_second(h, jnp.concatenate([v, rest], axis=0), n_t > 2)
+                v = jnp.concatenate([v, rest], axis=0)
+                col_out2[h] = edge(v).astype(bf16)
+                t = jnp.concatenate([jnp.zeros((X, C), f32), v[2 * (H - 1)], v[:6].reshape(6 * X, C)], axis=0)
+                t = t.astype(bf16)
+                high = t[:, LANES:]
+                lo2[1, h, 2 * T : 4 * T] = t[T : 3 * T, :LANES]
+                hc2[h, T : 4 * T] = jnp.concatenate([high[: 3 * T], high[T:]], axis=1)
             if n_t > 2:
-                put_tail_cols(tail2.at[pl.ds(0, R - 2)], tailc2)
-                put_tail_cols(tail2.at[pl.ds(R - 2, 4)], taile2)
-                later(tails_second((6, 7, 9, 10)))
+                @pl.when(me_t < n_t - 1)
+                def _():
+                    put_tails(range(2, R), 0, R - 2, tailc2)
+                    put_tails(ends, R - 2, 4, taile2)
+                    later(tails_second((6, 7, 9, 10)))
 
     col_copy(False).start()
 
@@ -492,7 +523,7 @@
 def shards(sizes, features, frame_counts, gain_first, conv_first, bias_first, gain_second, conv_second, bias_second):
     F, R, X, C = features.shape
     n_t, n_z, n_w = sizes
-    assert n_w == 2 and F % 2 == 0 and F >= 4 and X == 8 and 2 * (C - LANES) == LANES and R >= 4
+    assert n_w == 2 and F % 2 == 0 and F >= 6 and X == 8 and 2 * (C - LANES) == LANES and R >= 4
     H = F // 2
     S, T = F * X, 2 * X
     inner = -(-(R - 2) // 8) * 8

time: 12.8 us -> 12.6 us (0.984)
  Pallas kernels: 11.3 us -> 11 us
    pallas_call x1, Pallas kernels: 11.3 us -> 11 us  [shards(): pl.pallas_call(functools.partial(kernel, sizes), out_shape=pltpu.VMEM(fea...]
where the time goes in v4:
time: 12.6 us; the launch traced here: 12.4 us
  Pallas kernels  11 us (87%)
  local copies, waits for them, and re-layouts  0.71 us (6%)
  between operations  0.66 us (5%)
    pallas_call x1, Pallas kernels, shards(): pl.pallas_call(functools.partial(kernel, sizes), out_shape=pltpu.VMEM(fea...  11 us
    unnamed x1, local copies, waits for them, and re-layouts  0.71 us

profile of v4, /device:TPU:15, one launch (start us, length us, event | category | flops | bytes accessed | tf_op | source)
XLA Modules:
  0.0 12.4 jit_solution(16364695142223990414)
XLA Ops:
  0.7 11.0 %shard_map.82 = bf16[8,8,8,192]{3,2,1,0:T(8,128)(2,1)S(1)} custom-call(s32[1]{0:T(128)S(6)} %copy.11.refs_0_, bf16[8,8,8,192]{3,2,1,0:T(8,128)(2,1)} %refs_1_.1, f32[1,192]{1,0:T(1,128)} %bitcast.4, bf16[3,3,3,192,192]{4,3,2,1,0:T(8,128)(2,1)} %refs_3_.1, f32[1,192]{1,0:T(1,128)} %bitcast.5, f32[1,192]{1,0:T(1,128)} %bitcast.6, ...), custom_call_target="tpu_custom_call" | custom-call | tf_op jit(solution)/shard_map/pallas_call | solution.py:582
  11.7 0.7 %copy.10 = bf16[8,8,8,192]{3,2,1,0:T(8,128)(2,1)} copy(bf16[8,8,8,192]{3,2,1,0:T(8,128)(2,1)S(1)} %shard_map.82) | data formatting | bytes 393216

commit v5 on v4

--- a/solution.py
+++ b/solution.py
@@ -242,24 +242,34 @@
             acc[pl.ds(y0 * S, n * S)] = got
 
     def before(first, n, wl, wc, ws):
-        carry[...] = jnp.zeros(carry.shape, f32)
-        carry_col[...] = jnp.zeros(carry_col.shape, f32)
-        for k in range(n_t - 1):
+        tail_in = tail_in1 if first else tail_in2
+        col_refs = (tailc_in1, tailhc_in.at[:, 0], tailhc_in.at[:, 1]) if first else (tailc_in2, taile_in2)
+
+        def arrive(k):
+            for i in (8, 0, 1) if first else (6, 7, 9, 10):
+                far(k, k, i).wait_recv()
+            if first:
+                @pl.when(has[0])
+                def _():
+                    for i in (4, 5):
+                        far(k, k, i, -1).wait_recv()
+
+                @pl.when(has[1])
+                def _():
+                    for i in (2, 3):
+                        far(k, k, i, -1).wait_recv()
+
+        arrive(0)
+        if n_t > 2:
+            for at in range(n + 2):
+                carry[at] = tail_in[0, at].astype(f32)
+            for d, ref in enumerate(col_refs):
+                late = ref[0].astype(f32)
+                carry_col[d, :, : late.shape[1]] = late
+        for k in range(1, n_t - 1):
             @pl.when(me_t > k)
             def _(k=k):
-                for i in (8, 0, 1) if first else (6, 7, 9, 10):
-                    far(k, k, i).wait_recv()
-                if first:
-                    @pl.when(has[0])
-                    def _():
-                        for i in (4, 5):
-                            far(k, k, i, -1).wait_recv()
-
-                    @pl.when(has[1])
-                    def _():
-                        for i in (2, 3):
-                            far(k, k, i, -1).wait_recv()
-
+                arrive(k)
                 total = cnt_in[k]
 
                 def merge(total, early0, early1, late0, late1):
@@ -270,17 +280,20 @@
                     )
 
                 for at in range(n + 2):
-                    late = (tail_in1 if first else tail_in2)[k, at].astype(f32)
+                    late = tail_in[k, at].astype(f32)
                     got = merge(total, carry[at, :X], carry[at, X:], late[:X], late[X:])
                     carry[at] = jnp.concatenate(got, axis=0)
-                cols = (tailc_in1.at[k], tailhc_in.at[k, 0], tailhc_in.at[k, 1]) if first else (tailc_in2.at[k], taile_in2.at[k])
-                for d, ref in enumerate(cols):
-                    late = ref[...].astype(f32)
+                for d, ref in enumerate(col_refs):
+                    late = ref[k].astype(f32)
                     there = pl.ds(0, late.shape[1])
                     got = merge(total[:1], carry_col[d, 0, there], carry_col[d, 1, there], late[0], late[1])
                     carry_col[d, 0, there] = got[0]
                     carry_col[d, 1, there] = got[1]
 
+        if n_t > 2:
+            cols = [carry_col[d] for d in range(len(col_refs))]
+        else:
+            cols = [ref[0].astype(f32) for ref in col_refs]
         zero = jnp.zeros((X, C), f32)
         for yy in range(n + 2):
             at = slot_of(yy)
@@ -292,8 +305,8 @@
                     at, d, y = yy - 2, 0, yy - 2
                 else:
                     d, y = 2, yy - R - 2
-            col = jnp.concatenate([carry_col[d, f, y : y + 1] for f in range(2)], axis=0)
-            v = carry[at].reshape(2, X, C)
+            col = jnp.concatenate([cols[d][f, y : y + 1] for f in range(2)], axis=0)
+            v = (carry[at] if n_t > 2 else tail_in[0, at].astype(f32)).reshape(2, X, C)
             left, right = beside(v, col)
             made = []
             for j, b in enumerate((left, v, right)):

time: 12.6 us -> 12.5 us (level)
  no operation moved by 1% of the time
where the time goes in v5:
time: 12.5 us; the launch traced here: 12.4 us
  Pallas kernels  11 us (88%)
  local copies, waits for them, and re-layouts  0.71 us (6%)
  between operations  0.66 us (5%)
    pallas_call x1, Pallas kernels, shards(): pl.pallas_call(functools.partial(kernel, sizes), out_shape=pltpu.VMEM(fea...  11 us
    unnamed x1, local copies, waits for them, and re-layouts  0.71 us

profile of v5, /device:TPU:15, one launch (start us, length us, event | category | flops | bytes accessed | tf_op | source)
XLA Modules:
  0.0 12.4 jit_solution(12316239192015441922)
XLA Ops:
  0.7 11.0 %shard_map.82 = bf16[8,8,8,192]{3,2,1,0:T(8,128)(2,1)S(1)} custom-call(s32[1]{0:T(128)S(6)} %copy.11.refs_0_, bf16[8,8,8,192]{3,2,1,0:T(8,128)(2,1)} %refs_1_.1, f32[1,192]{1,0:T(1,128)} %bitcast.4, bf16[3,3,3,192,192]{4,3,2,1,0:T(8,128)(2,1)} %refs_3_.1, f32[1,192]{1,0:T(1,128)} %bitcast.5, f32[1,192]{1,0:T(1,128)} %bitcast.6, ...), custom_call_target="tpu_custom_call" | custom-call | tf_op jit(solution)/shard_map/pallas_call | solution.py:595
  11.6 0.7 %copy.10 = bf16[8,8,8,192]{3,2,1,0:T(8,128)(2,1)} copy(bf16[8,8,8,192]{3,2,1,0:T(8,128)(2,1)S(1)} %shard_map.82) | data formatting | bytes 393216
